TPU v7x, 32 devices: a whole 2x2x4 slice. The times are simulated.
32 devices in a mesh: section: 4 (over z), vit: 2 (over x), dp: 4 (over y, core).
Axes of the slice: x: 2, y: 2, z: 4, core: 2. Of those that a mesh axis runs over, the one named last changes fastest.
Arguments:
- grad_llm: bfloat16 [4, 1024, 4096], P('section', ('dp', 'vit')), parts along dimension 1, may hold values from -6 to 6
- vis_slot: int32 [8, 128], P('dp'), parts along dimension 0, may hold values from 0 to 255, as said below
- image_rows: int32 [16, 2], P('dp'), parts along dimension 0, may hold values from 8 to 32, as said below
- section_layer: int32 [4], replicated, may hold values from 0 to 3, each once
- vit_in: bfloat16 [4096, 1152], P(('dp', 'section', 'vit')), parts along dimension 0, may hold values from -6 to 6
- vit_out: bfloat16 [4096, 1152], P(('dp', 'section', 'vit')), parts along dimension 0, may hold values from -6 to 6
- ln_gain: float32 [1152], replicated, may hold values from 0.5 to 1.5
- ln_bias: float32 [1152], replicated, may hold values from -3 to 3
- qkv_weight: bfloat16 [1152, 3456], P('section'), may hold values from -0.1875 to 0.1875
- proj_weight: bfloat16 [1152, 1152], P('section'), may hold values from -0.1875 to 0.1875
- merge_gain: float32 [1152], replicated, may hold values from 0.5 to 1.5
- merge_bias: float32 [1152], replicated, may hold values from -3 to 3
- fc1_weight: bfloat16 [4608, 4608], P(None, 'vit'), may hold values from -0.09375 to 0.09375
- fc1_bias: float32 [4608], P('vit'), may hold values from -3 to 3
- fc2_weight: bfloat16 [4608, 4096], P('vit'), may hold values from -0.09375 to 0.09375
Outputs:
- vit_grad: bfloat16 [4096, 1152], P(('dp', 'section', 'vit')), parts along dimension 0
There are 4 independent parts, one for each index of `dp`. A program takes and returns all parts, laid end to end along the dimension named above; an argument that names none is the same for every part. Nothing has to cross between parts.
Inputs may be any that keep to these rules, and one draw needn't show every extreme that they name: `vis_slot`: every slot number appears once. On every language-model device v, the rows d * 16 to d * 16 + 15 name 16 consecutive slots that start at a multiple of 16 inside d * 32 to d * 32 + 31, the slots of vision device d (devices numbered with the group first). `image_rows`: in every group one image has exactly 32 merged tokens. `section_layer`: A permutation; the section with value 3 holds no DeepStack layer.
All inputs are finite; a program needn't handle non-finite values.
Results may differ from a plain program's by a relative error of at most 0.02.
Values may be sent and summed in bfloat16 or wider, within the bound.
No kernel may reach another device: no remote copies, remote signals or barrier semaphores. Data moves between devices by JAX's collectives and lax.ppermute only.
A program may use at most 128 MiB of HBM per device.

v0:
```python
import jax
import jax.numpy as jnp
from jax import lax
from jax.sharding import PartitionSpec as P

HEADS = 16
LEVELS = 3
norm_eps = 1e-06


def normalize(values):
    row_mean = jnp.mean(values, axis=-1, keepdims=True)
    centered = values - row_mean
    variance = jnp.mean(centered * centered, axis=-1, keepdims=True)
    inverse = lax.rsqrt(variance + norm_eps)
    return (centered * inverse, inverse)


def normalize_back(upstream, normed_rows, inverse, gain):
    scaled = upstream * gain
    mean_scaled = jnp.mean(scaled, axis=-1, keepdims=True)
    mean_cross = jnp.mean(scaled * normed_rows, axis=-1, keepdims=True)
    return (scaled - mean_scaled - normed_rows * mean_cross) * inverse


def gelu_slope(pre_act):
    cumulative = 0.5 * (1.0 + lax.erf(pre_act * 0.7071067811865476))
    density = jnp.exp(-0.5 * pre_act * pre_act) * 0.3989422804014327
    return cumulative + pre_act * density


def local(
    grad_llm,
    vis_slot,
    image_rows,
    section_layer,
    vit_in,
    vit_out,
    ln_gain,
    ln_bias,
    qkv_weight,
    proj_weight,
    merge_gain,
    merge_bias,
    fc1_weight,
    fc1_bias,
    fc2_weight,
):
    sections = lax.axis_size("section")
    shards = lax.axis_size("vit")
    section_index = lax.axis_index("section")
    shard_index = lax.axis_index("vit")
    devices = sections * shards
    patches = vit_in.shape[0]
    slots_here = patches // 4
    run_rows = grad_llm.shape[1] // devices
    llm_width = grad_llm.shape[2]
    vit_width = vit_in.shape[1]
    head_dim = vit_width // HEADS
    device_index = section_index * shards + shard_index
    qkv_full, proj_full = (
        lax.all_gather(qkv_weight, "section", axis=0, tiled=True),
        lax.all_gather(proj_weight, "section", axis=0, tiled=True),
    )
    in_rows, in_inverse = normalize(vit_in.astype(jnp.float32))
    normed = (in_rows * ln_gain + ln_bias).astype(jnp.bfloat16)
    projected = lax.dot_general(
        qkv_full, normed, (((0,), (1,)), ((), ())), preferred_element_type=jnp.float32
    )
    projected = projected.astype(jnp.bfloat16).reshape(3, HEADS, head_dim, patches)
    section_weight = jnp.where(
        section_layer < LEVELS, (section_layer + 1).astype(jnp.float32) / LEVELS, 0.0
    )
    outgoing = grad_llm[0].reshape(devices, run_rows, llm_width)
    image_ends = jnp.cumsum(image_rows[section_index])
    out_rows, out_inverse = normalize(vit_out.astype(jnp.float32))
    merge_in = (
        (out_rows * merge_gain + merge_bias).astype(jnp.bfloat16).reshape(slots_here, 4 * vit_width)
    )
    arrived = lax.all_to_all(outgoing, ("section", "vit"), split_axis=0, concat_axis=0, tiled=True)
    arrived_f = arrived.reshape(sections, shards, run_rows, llm_width).astype(jnp.float32)
    incoming = jnp.sum(arrived_f * section_weight[:, None, None, None], axis=0)
    columns = lax.dynamic_slice_in_dim(vis_slot, device_index * run_rows, run_rows, 1)
    local_slot = (columns - device_index * slots_here).reshape(-1)
    placed = (
        jnp.zeros((slots_here, llm_width), jnp.float32)
        .at[local_slot]
        .set(incoming.reshape(-1, llm_width))
    )
    slot_position = shard_index * slots_here + jnp.arange(slots_here, dtype=jnp.int32)
    merged_grad = jnp.where((slot_position < image_ends[-1])[:, None], placed, 0.0).astype(
        jnp.bfloat16
    )
    rows_in, rows_grad = (
        lax.all_gather(merge_in, "vit", axis=0, tiled=True),
        lax.all_gather(merged_grad, "vit", axis=0, tiled=True),
    )
    pre_act = jnp.dot(rows_in, fc1_weight, preferred_element_type=jnp.float32) + fc1_bias
    hidden_grad = lax.dot_general(
        rows_grad, fc2_weight, (((1,), (1,)), ((), ())), preferred_element_type=jnp.float32
    )
    pre_grad = (hidden_grad * gelu_slope(pre_act)).astype(jnp.bfloat16)
    merge_grad = lax.psum_scatter(
        lax.dot_general(
            pre_grad, fc1_weight, (((1,), (1,)), ((), ())), preferred_element_type=jnp.float32
        ).astype(jnp.bfloat16),
        "vit",
        scatter_dimension=0,
        tiled=True,
    ).astype(jnp.float32)
    out_grad = normalize_back(
        merge_grad.reshape(patches, vit_width), out_rows, out_inverse, merge_gain
    ).astype(jnp.bfloat16)
    grad_cols = lax.dot_general(
        proj_full, out_grad, (((1,), (1,)), ((), ())), preferred_element_type=jnp.float32
    )
    grad_cols = grad_cols.astype(jnp.bfloat16).reshape(1, HEADS, head_dim, patches)
    head_inputs, head_grad = (
        lax.all_to_all(projected, "vit", split_axis=1, concat_axis=3, tiled=True),
        lax.all_to_all(grad_cols, "vit", split_axis=1, concat_axis=3, tiled=True),
    )
    length = shards * patches
    block_size = min(512, length)
    block_count = length // block_size
    slot_of = jnp.arange(length, dtype=jnp.int32) // 4
    patch_image = jnp.sum((slot_of[:, None] >= image_ends[None, :]).astype(jnp.int32), axis=1)
    patch_live = slot_of < image_ends[-1]
    score_scale = head_dim ** (-0.5)
    contract_first = (((0,), (0,)), ((), ()))

    def head_backward(query_cols, key_cols, value_cols, grad_head):

        def step(carry, block_index):
            key_acc, value_acc = carry
            first_row = block_index * block_size
            query_block = lax.dynamic_slice_in_dim(query_cols, first_row, block_size, 1)
            grad_block = lax.dynamic_slice_in_dim(grad_head, first_row, block_size, 1)
            image_block = lax.dynamic_slice_in_dim(patch_image, first_row, block_size, 0)
            live_block = lax.dynamic_slice_in_dim(patch_live, first_row, block_size, 0)
            scores = (
                lax.dot_general(
                    query_block, key_cols, contract_first, preferred_element_type=jnp.float32
                )
                * score_scale
            )
            allowed = (
                (image_block[:, None] == patch_image[None, :])
                & live_block[:, None]
                & patch_live[None, :]
            )
            exponent = jnp.where(allowed, jnp.exp(jnp.where(allowed, scores, 0.0)), 0.0)
            denominator = (
                jnp.sum(exponent, axis=1, keepdims=True)
                + 1.0
                - live_block.astype(jnp.float32)[:, None]
            )
            softmax_weights = (exponent / denominator).astype(jnp.bfloat16)
            prob_grad = lax.dot_general(
                grad_block, value_cols, contract_first, preferred_element_type=jnp.float32
            )
            weighted = softmax_weights.astype(jnp.float32)
            row_dot = jnp.sum(weighted * prob_grad, axis=1, keepdims=True)
            score_grad = (weighted * (prob_grad - row_dot) * score_scale).astype(jnp.bfloat16)
            query_grad = lax.dot_general(
                key_cols, score_grad, (((1,), (1,)), ((), ())), preferred_element_type=jnp.float32
            )
            key_acc = key_acc + lax.dot_general(
                query_block,
                score_grad,
                (((1,), (0,)), ((), ())),
                preferred_element_type=jnp.float32,
            )
            value_acc = value_acc + lax.dot_general(
                grad_block,
                softmax_weights,
                (((1,), (0,)), ((), ())),
                preferred_element_type=jnp.float32,
            )
            return ((key_acc, value_acc), query_grad.astype(jnp.bfloat16))

        empty = jnp.zeros((head_dim, length), jnp.float32)
        (key_total, value_total), query_blocks = lax.scan(
            step, (empty, empty), jnp.arange(block_count, dtype=jnp.int32)
        )
        query_total = query_blocks.transpose(1, 0, 2).reshape(head_dim, length)
        return (query_total, key_total.astype(jnp.bfloat16), value_total.astype(jnp.bfloat16))

    query_all, key_all, value_all = jax.vmap(head_backward)(
        head_inputs[0], head_inputs[1], head_inputs[2], head_grad[0]
    )
    head_result = jnp.stack([query_all, key_all, value_all])
    returned = lax.all_to_all(head_result, "vit", split_axis=3, concat_axis=1, tiled=True)
    projected_grad = returned.reshape(3 * vit_width, patches)
    normed_grad = lax.dot_general(
        projected_grad, qkv_full, (((0,), (1,)), ((), ())), preferred_element_type=jnp.float32
    )
    vit_grad = out_grad.astype(jnp.float32) + normalize_back(
        normed_grad, in_rows, in_inverse, ln_gain
    )
    return vit_grad.astype(jnp.bfloat16)


def solution(mesh):
    placed = (
        P("section", ("dp", "vit"), None),
        P("dp", None),
        P("dp", None),
        P(),
        P(("dp", "section", "vit"), None),
        P(("dp", "section", "vit"), None),
        P(),
        P(),
        P("section", None),
        P("section", None),
        P(),
        P(),
        P(None, "vit"),
        P("vit"),
        P("vit", None),
    )
    return jax.shard_map(
        local,
        mesh=mesh,
        in_specs=placed,
        out_specs=P(("dp", "section", "vit"), None),
        check_vma=False,
    )
```

profile of v0, /device:TPU:0, one launch (start us, length us, event | category | flops | bytes accessed | tf_op | source)
XLA Modules:
  0.0 350.3 jit_solution(10939154692801934895)
XLA Ops:
  7.4 7.4 %all-to-all-start = ((bf16[8,16,4096]{2,1,0:T(8,128)(2,1)}), bf16[8,16,4096]{2,1,0:T(8,128)(2,1)S(1)}, u32[]{:S(2)}, u32[]{:S(2)}) async-start(bf16[8,16,4096]{2,1,0:T(8,128)(2,1)} %bitcast.69), calls=%async_computation | async-start | bytes 2097152 | tf_op jit(solution)/shard_map/all_to_all | solution.py:80
  14.8 0.0 reduce-scatter.2.cloned.1.call-start
  14.9 0.2 dynamic-slice_reduce_fusion
  15.1 0.2 reduce-window.4
  15.3 0.6 slice.17
  15.8 0.1 convert_reduce_fusion.1
  16.0 0.2 fusion.41
  16.2 0.1 dynamic-slice_subtract_fusion
  16.3 0.2 fusion.36
  16.6 0.7 add_compare_fusion
  17.2 0.1 reshape.192
  17.3 0.2 reshape.194
  17.5 16.7 %all_gather.13 = bf16[64,4608]{1,0:T(8,128)(2,1)S(1)} all-gather(bf16[32,4608]{1,0:T(8,128)(2,1)S(1)} %reshape.194), channel_id=1, replica_groups=mesh['section'=4,'vit'=2,'dp'=4] {'vit'}, dimensions={0}, use_global_device_ids=true | all-gather | bytes 884736 | tf_op jit(solution)/shard_map/all_gather | solution.py:95
  34.2 9.1 %convolution_add_fusion = f32[64,2304]{1,0:T(8,128)S(1)} fusion(bf16[64,4608]{1,0:T(8,128)(2,1)S(1)} %all_gather.13, bf16[4608,2304]{1,0:T(8,128)(2,1)} %param.27, f32[2304]{0:T(1024)S(1)} %copy-done.7), kind=kOutput, calls=%fused_computation.6 | convolution fusion | flops 1359101952 | bytes 22422528 | tf_op jit(solution)/shard_map/dot_general | solution.py:98
  43.3 0.3 fusion.6
  43.6 1.0 scatter_custom_fusion
  44.6 0.1 select_convert_fusion
  44.7 7.5 %all_gather.12 = bf16[64,4096]{1,0:T(8,128)(2,1)S(1)} all-gather(bf16[32,4096]{1,0:T(8,128)(2,1)S(1)} %select_convert_fusion), channel_id=1, replica_groups=mesh['section'=4,'vit'=2,'dp'=4] {'vit'}, dimensions={0}, use_global_device_ids=true | all-gather | bytes 786432 | tf_op jit(solution)/shard_map/all_gather | solution.py:96
  52.2 20.2 %convolution_convert_fusion = bf16[64,4608]{1,0:T(8,128)(2,1)} fusion(bf16[4608,2304]{1,0:T(8,128)(2,1)} %param.27, bf16[64,4096]{1,0:T(8,128)(2,1)S(1)} %all_gather.12, bf16[2304,4096]{1,0:T(8,128)(2,1)} %param.29, f32[64,2304]{1,0:T(8,128)S(1)} %convolution_add_fusion), kind=kOutput, calls=%fused_computation.2 | convolution fusion | flops 2568683520 | bytes 41811968 | tf_op jit(solution)/shard_map/dot_general | solution.py:104
  72.3 0.0 reduce-scatter.2.cloned.1.call-update
  72.4 0.0 all-gather.5.cloned.1.call-start
  72.4 0.5 all-gather.5.cloned.1.call-update
  72.9 0.0 all-gather.3.cloned.1.call-start
  73.0 0.5 all-gather.3.cloned.1.call-update
  73.5 0.7 broadcast_compare_fusion
  74.2 0.1 convert_reduce_fusion
  74.3 0.2 fusion.34
  74.6 14.3 %reduce-scatter.2.cloned.1.call-done = bf16[32,4608]{1,0:T(8,128)(2,1)} async-done(((bf16[64,4608]{1,0:T(8,128)(2,1)}), bf16[32,4608]{1,0:T(8,128)(2,1)}) %reduce-scatter.2.cloned.1.call-update) | async-done | bytes 294928 | tf_op jit(solution)/shard_map/reduce_scatter | solution.py:103
  88.9 1.1 reshape.204
  90.0 0.2 multiply_reduce_fusion
  90.3 40.3 %all-gather.5.cloned.1.call-done = bf16[1152,1152]{1,0:T(8,128)(2,1)} async-done(((bf16[288,1152]{1,0:T(8,128)(2,1)}), bf16[1152,1152]{1,0:T(8,128)(2,1)}) %all-gather.5.cloned.1.call-update) | async-done | bytes 2654224 | tf_op jit(solution)/shard_map/all_gather | solution.py:63
  130.6 2.7 fusion.3
  133.3 0.9 copy.54
  134.2 3.5 all-to-all-start.2
  137.7 135.5 %all-gather.3.cloned.1.call-done = bf16[1152,3456]{1,0:T(8,128)(2,1)} async-done(((bf16[288,3456]{1,0:T(8,128)(2,1)}), bf16[1152,3456]{1,0:T(8,128)(2,1)}) %all-gather.3.cloned.1.call-update) | async-done | bytes 7962640 | tf_op jit(solution)/shard_map/all_gather | solution.py:62
  273.2 4.7 %fusion.1 = bf16[3456,128]{0,1:T(8,128)(2,1)S(1)} fusion(bf16[1152,3456]{1,0:T(8,128)(2,1)} %all-gather.3.cloned.1.call-done, bf16[128,1152]{1,0:T(8,128)(2,1)S(1)} %copy-done.3, f32[1152]{0:T(1024)S(1)} %copy-done.8, f32[1152]{0:T(1024)S(1)} %copy-done.6, f32[128]{0:T(128)S(1)} %add_rsqrt_fusion, f32[128]{0:T(128)S(1)} %broadcast_multiply_fusion.2), kind=kOutput, calls=%fused_computation.4 | convolution fusion | flops 1020542976 | bytes 9152512 | tf_op jit(solution)/shard_map/dot_general | solution.py:67
  278.0 1.0 copy.51
  279.0 1.1 copy.52
  280.1 3.7 %all-to-all-start.1 = ((bf16[3,16,72,128]{3,2,0,1:T(8,128)(2,1)}), bf16[3,16,72,128]{3,2,0,1:T(8,128)(2,1)S(1)}, u32[]{:S(2)}, u32[]{:S(2)}) async-start(bf16[3,16,72,128]{3,2,0,1:T(8,128)(2,1)} %copy.52), calls=%async_computation.2 | async-start | bytes 1769472 | tf_op jit(solution)/shard_map/all_to_all | solution.py:119
  283.8 0.1 fusion.53
  283.9 0.1 and_and_fusion
  284.0 0.3 copy.70
  284.4 0.2 reshape.201
  284.6 11.3 %all-to-all-done.1 = bf16[3,16,72,128]{3,2,0,1:T(8,128)(2,1)S(1)} async-done(((bf16[3,16,72,128]{3,2,0,1:T(8,128)(2,1)}), bf16[3,16,72,128]{3,2,0,1:T(8,128)(2,1)S(1)}, u32[]{:S(2)}, u32[]{:S(2)}) %all-to-all-start.1) | async-done | bytes 884768 | tf_op jit(solution)/shard_map/all_to_all | solution.py:119
  295.9 0.9 copy.69
  296.8 0.6 fusion.62
  297.4 0.2 reshape.200
  297.6 0.2 squeeze.21
  297.8 0.0 copy-start.4
  297.8 0.2 squeeze.24
  298.0 0.7 fusion.63
  298.8 0.2 divide_convert_fusion
  299.0 0.4 fusion.14
  299.4 1.9 fusion.64
  301.3 3.0 fusion.12
  304.3 3.1 fusion.13
  307.4 1.1 pad_maximum_fusion
  308.5 1.9 copy.60
  310.4 22.2 %all_to_all.50 = bf16[3,8,72,256]{2,1,0,3:T(8,128)(2,1)} all-to-all(bf16[3,8,72,256]{2,1,0,3:T(8,128)(2,1)S(1)} %copy.60), channel_id=1, replica_groups=mesh['section'=4,'vit'=2,'dp'=4] {'vit'}, dimensions={3} | all-to-all | bytes 1769472 | tf_op jit(solution)/shard_map/all_to_all | solution.py:192
  332.6 3.0 copy.66
  335.6 0.1 copy.62
  335.7 0.0 copy-start.1
  335.7 6.0 %fusion.61 = (f32[128]{0:T(128)S(1)}, f32[128]{0:T(128)S(1)}, f32[128,1152]{1,0:T(8,128)S(1)}) fusion(f32[128]{0:T(128)S(1)} %add_rsqrt_fusion, f32[128]{0:T(128)S(1)} %broadcast_multiply_fusion.2, bf16[128,1152]{1,0:T(8,128)(2,1)S(1)} %copy-done.3, f32[1152]{0:T(1024)S(1)} %copy-done.6, bf16[3456,128]{1,0:T(8,128)(2,1)S(1)} %bitcast.62, ...), kind=kOutput, calls=%fused_computation.103 | convolution fusion | flops 1020247808 | bytes 9738752 | tf_op jit(solution)/shard_map/dot_general | solution.py:194
  341.7 1.1 fusion.33
  (35 shorter events, 0.1 us)
Async XLA Ops:
  7.4 7.5 %copy-start = (s32[4,2]{0,1:T(2,128)S(1)}, s32[4,2]{0,1:T(2,128)}, u32[]{:S(2)}) copy-start(s32[4,2]{0,1:T(2,128)} %param.17) | copy-start | bytes 100
  7.4 8.5 %copy-start.2 = (bf16[128,1152]{1,0:T(8,128)(2,1)S(1)}, bf16[128,1152]{1,0:T(8,128)(2,1)}, u32[]{:S(2)}) copy-start(bf16[128,1152]{1,0:T(8,128)(2,1)} %param.20) | copy-start | bytes 884740
  7.4 8.8 %copy-start.10 = (s32[2,128]{1,0:T(2,128)S(1)}, s32[2,128]{1,0:T(2,128)}, u32[]{:S(2)}) copy-start(s32[2,128]{1,0:T(2,128)} %param.16) | copy-start | bytes 3076
  7.4 8.9 %copy-start.9 = (f32[1152]{0:T(1024)S(1)}, f32[1152]{0:T(1024)}, u32[]{:S(2)}) copy-start(f32[1152]{0:T(1024)} %param.26) | copy-start | bytes 13828
  7.4 8.9 %copy-start.5 = (f32[1152]{0:T(1024)S(1)}, f32[1152]{0:T(1024)}, u32[]{:S(2)}) copy-start(f32[1152]{0:T(1024)} %param.25) | copy-start | bytes 13828
  7.4 26.8 %copy-start.11 = (s32[4]{0:T(128)S(1)}, s32[4]{0:T(128)}, u32[]{:S(2)}) copy-start(s32[4]{0:T(128)} %param.18) | copy-start | bytes 52
  7.4 26.8 %copy-start.7 = (f32[2304]{0:T(1024)S(1)}, f32[2304]{0:T(1024)}, u32[]{:S(2)}) copy-start(f32[2304]{0:T(1024)} %param.28) | copy-start | bytes 27652
  7.4 35.8 %all-to-all-start = ((bf16[8,16,4096]{2,1,0:T(8,128)(2,1)}), bf16[8,16,4096]{2,1,0:T(8,128)(2,1)S(1)}, u32[]{:S(2)}, u32[]{:S(2)}) async-start(bf16[8,16,4096]{2,1,0:T(8,128)(2,1)} %bitcast.69), calls=%async_computation | async-start | bytes 2097152 | tf_op jit(solution)/shard_map/all_to_all | solution.py:80
  14.8 74.0 %reduce-scatter.2.cloned.1.call-start = ((), (), s32[]{:S(2)}) async-start(), calls=%async_computation.5 | async-start | bytes 884736 | tf_op jit(solution)/shard_map/reduce_scatter | solution.py:103
  72.3 1.9 copy-start.3
  72.4 58.2 %all-gather.5.cloned.1.call-start = ((), (), s32[]{:S(2)}) async-start(), calls=%async_computation.7 | async-start | bytes 3317760 | tf_op jit(solution)/shard_map/all_gather | solution.py:63
  72.9 200.3 %all-gather.3.cloned.1.call-start = ((), (), s32[]{:S(2)}) async-start(), calls=%async_computation.6 | async-start | bytes 9953280 | tf_op jit(solution)/shard_map/all_gather | solution.py:62
  130.6 142.6 %copy-start.6 = (f32[1152]{0:T(1024)S(1)}, f32[1152]{0:T(1024)}, u32[]{:S(2)}) copy-start(f32[1152]{0:T(1024)} %param.21) | copy-start | bytes 13828
  130.6 142.6 %copy-start.8 = (f32[1152]{0:T(1024)S(1)}, f32[1152]{0:T(1024)}, u32[]{:S(2)}) copy-start(f32[1152]{0:T(1024)} %param.22) | copy-start | bytes 13828
  134.2 145.8 %all-to-all-start.2 = ((bf16[1,16,72,128]{3,2,0,1:T(8,128)(2,1)}), bf16[1,16,72,128]{3,2,0,1:T(8,128)(2,1)S(1)}, u32[]{:S(2)}, u32[]{:S(2)}) async-start(bf16[1,16,72,128]{3,2,0,1:T(8,128)(2,1)} %bitcast.12), calls=%async_computation.3 | async-start | bytes 589824 | tf_op jit(solution)/shard_map/all_to_all | solution.py:120
  280.1 15.8 %all-to-all-start.1 = ((bf16[3,16,72,128]{3,2,0,1:T(8,128)(2,1)}), bf16[3,16,72,128]{3,2,0,1:T(8,128)(2,1)S(1)}, u32[]{:S(2)}, u32[]{:S(2)}) async-start(bf16[3,16,72,128]{3,2,0,1:T(8,128)(2,1)} %copy.52), calls=%async_computation.2 | async-start | bytes 1769472 | tf_op jit(solution)/shard_map/all_to_all | solution.py:119
  297.8 0.9 copy-start.4
  335.7 7.2 %copy-start.1 = (s32[4,2]{0,1:T(2,128)S(1)}, s32[4,2]{0,1:T(2,128)}, u32[]{:S(2)}) copy-start(s32[4,2]{0,1:T(2,128)} %param.17) | copy-start | bytes 100
Sparse Core Ops, SparseCore 0:
  72.5 16.3 reduce-scatter.1
Sparse Core Ops, SparseCore 1:
  74.4 56.1 all-gather.4
  132.1 141.1 all-gather.2
where the time goes:
time: 351 us; the launch traced here: 350 us
  waiting for transfers between devices  203 us (58%)
  matrix products  51.8 us (15%)
  blocking collectives  46.3 us (13%)
  between operations  15.2 us (4%)
  starting transfers between devices  14.8 us (4%)
  local copies, waits for them, and re-layouts  13.8 us (4%)
  other arithmetic  5.89 us (2%)
    all_gather x1, waiting for transfers between devices, local(): lax.all_gather(qkv_weight, 'section', axis=0, tiled=True)  136 us
    all_gather x1, waiting for transfers between devices, local(): lax.all_gather(proj_weight, 'section', axis=0, tiled=True)  40.3 us
    all_to_all x1, blocking collectives, local(): lax.all_to_all(head_result, 'vit', split_axis=3, concat_axis=1, tiled=True)  22.2 us
    dot_general x1, matrix products, local(): lax.dot_general(pre_grad, fc1_weight, (((1,), (1,)), ((), ())), preferred...  20.2 us
    all_gather x1, blocking collectives, local(): lax.all_gather(merge_in, 'vit', axis=0, tiled=True)  16.7 us
    reduce_scatter x1, waiting for transfers between devices, local(): lax.psum_scatter(lax.dot_general(pre_grad, fc1_weight, (((1,), (1,)), (()...  14.3 us
    all_to_all x1, waiting for transfers between devices, local(): lax.all_to_all(projected, 'vit', split_axis=1, concat_axis=3, tiled=True)  11.3 us
    dot_general x1, matrix products, local(): jnp.dot(rows_in, fc1_weight, preferred_element_type=jnp.float32) + fc1_bias  9.08 us
  transfers between devices with their start and end apart: 6, of which 4 were waited for; matrix products, arithmetic and copies ran while one was open for 7% of the time, Pallas kernels for 0%

commit v1 on v0

--- a/solution.py
+++ b/solution.py
@@ -2,6 +2,7 @@
 import jax.numpy as jnp
 from jax import lax
 from jax.sharding import PartitionSpec as P
+from jax.lax import all_to_all, axis_size
 
 HEADS = 16
 LEVELS = 3
@@ -189,7 +190,12 @@
         head_inputs[0], head_inputs[1], head_inputs[2], head_grad[0]
     )
     head_result = jnp.stack([query_all, key_all, value_all])
-    returned = lax.all_to_all(head_result, "vit", split_axis=3, concat_axis=1, tiled=True)
+    returned = jnp.concatenate(
+        all_to_all(
+            jnp.stack(jnp.split(head_result, axis_size("vit"), axis=3), axis=0), "vit", 0, 0
+        ),
+        axis=1,
+    )
     projected_grad = returned.reshape(3 * vit_width, patches)
     normed_grad = lax.dot_general(
         projected_grad, qkv_full, (((0,), (1,)), ((), ())), preferred_element_type=jnp.float32

time: 351 us -> 337 us (0.960)
  blocking collectives: 46.3 us -> 38 us
  local copies, waits for them, and re-layouts: 13.8 us -> 9.03 us
    all_to_all x1, blocking collectives: 22.2 us -> 13.9 us  [local(): all_to_all(jnp.stack(jnp.split(head_result, axis_size('vit'), axis=3), ax...]
where the time goes in v1:
time: 337 us; the launch traced here: 336 us
  waiting for transfers between devices  203 us (60%)
  matrix products  51.8 us (15%)
  blocking collectives  38 us (11%)
  between operations  15.2 us (5%)
  starting transfers between devices  14.8 us (4%)
  local copies, waits for them, and re-layouts  9.03 us (3%)
  other arithmetic  4.95 us (1%)
    all_gather x1, waiting for transfers between devices, local(): lax.all_gather(qkv_weight, 'section', axis=0, tiled=True)  136 us
    all_gather x1, waiting for transfers between devices, local(): lax.all_gather(proj_weight, 'section', axis=0, tiled=True)  40.3 us
    dot_general x1, matrix products, local(): lax.dot_general(pre_grad, fc1_weight, (((1,), (1,)), ((), ())), preferred...  20.2 us
    all_gather x1, blocking collectives, local(): lax.all_gather(merge_in, 'vit', axis=0, tiled=True)  16.7 us
    reduce_scatter x1, waiting for transfers between devices, local(): lax.psum_scatter(lax.dot_general(pre_grad, fc1_weight, (((1,), (1,)), (()...  14.3 us
    all_to_all x1, blocking collectives, local(): all_to_all(jnp.stack(jnp.split(head_result, axis_size('vit'), axis=3), ax...  13.9 us
    all_to_all x1, waiting for transfers between devices, local(): lax.all_to_all(projected, 'vit', split_axis=1, concat_axis=3, tiled=True)  11.3 us
    dot_general x1, matrix products, local(): jnp.dot(rows_in, fc1_weight, preferred_element_type=jnp.float32) + fc1_bias  9.08 us
  transfers between devices with their start and end apart: 6, of which 4 were waited for; matrix products, arithmetic and copies ran while one was open for 7% of the time, Pallas kernels for 0%

profile of v1, /device:TPU:0, one launch (start us, length us, event | category | flops | bytes accessed | tf_op | source)
XLA Modules:
  0.0 336.3 jit_solution(12052647936396391410)
XLA Ops:
  7.4 7.4 %all-to-all-start = ((bf16[8,16,4096]{2,1,0:T(8,128)(2,1)}), bf16[8,16,4096]{2,1,0:T(8,128)(2,1)S(1)}, u32[]{:S(2)}, u32[]{:S(2)}) async-start(bf16[8,16,4096]{2,1,0:T(8,128)(2,1)} %bitcast.71), calls=%async_computation | async-start | bytes 2097152 | tf_op jit(solution)/shard_map/all_to_all | solution.py:81
  14.8 0.0 reduce-scatter.2.cloned.1.call-start
  14.9 0.2 dynamic-slice_reduce_fusion
  15.1 0.2 reduce-window.4
  15.3 0.6 slice.17
  15.8 0.1 convert_reduce_fusion.1
  16.0 0.2 fusion.41
  16.2 0.1 dynamic-slice_subtract_fusion
  16.3 0.2 fusion.36
  16.6 0.7 add_compare_fusion
  17.2 0.1 reshape.191
  17.3 0.2 reshape.193
  17.5 16.7 %all_gather.13 = bf16[64,4608]{1,0:T(8,128)(2,1)S(1)} all-gather(bf16[32,4608]{1,0:T(8,128)(2,1)S(1)} %reshape.193), channel_id=1, replica_groups=mesh['section'=4,'vit'=2,'dp'=4] {'vit'}, dimensions={0}, use_global_device_ids=true | all-gather | bytes 884736 | tf_op jit(solution)/shard_map/all_gather | solution.py:96
  34.2 9.1 %convolution_add_fusion = f32[64,2304]{1,0:T(8,128)S(1)} fusion(bf16[64,4608]{1,0:T(8,128)(2,1)S(1)} %all_gather.13, bf16[4608,2304]{1,0:T(8,128)(2,1)} %param.27, f32[2304]{0:T(1024)S(1)} %copy-done.7), kind=kOutput, calls=%fused_computation.6 | convolution fusion | flops 1359101952 | bytes 22422528 | tf_op jit(solution)/shard_map/dot_general | solution.py:99
  43.3 0.3 fusion.6
  43.6 1.0 scatter_custom_fusion
  44.6 0.1 select_convert_fusion
  44.7 7.5 %all_gather.12 = bf16[64,4096]{1,0:T(8,128)(2,1)S(1)} all-gather(bf16[32,4096]{1,0:T(8,128)(2,1)S(1)} %select_convert_fusion), channel_id=1, replica_groups=mesh['section'=4,'vit'=2,'dp'=4] {'vit'}, dimensions={0}, use_global_device_ids=true | all-gather | bytes 786432 | tf_op jit(solution)/shard_map/all_gather | solution.py:97
  52.2 20.2 %convolution_convert_fusion = bf16[64,4608]{1,0:T(8,128)(2,1)} fusion(bf16[4608,2304]{1,0:T(8,128)(2,1)} %param.27, bf16[64,4096]{1,0:T(8,128)(2,1)S(1)} %all_gather.12, bf16[2304,4096]{1,0:T(8,128)(2,1)} %param.29, f32[64,2304]{1,0:T(8,128)S(1)} %convolution_add_fusion), kind=kOutput, calls=%fused_computation.2 | convolution fusion | flops 2568683520 | bytes 41811968 | tf_op jit(solution)/shard_map/dot_general | solution.py:105
  72.3 0.0 reduce-scatter.2.cloned.1.call-update
  72.4 0.0 all-gather.5.cloned.1.call-start
  72.4 0.5 all-gather.5.cloned.1.call-update
  72.9 0.0 all-gather.3.cloned.1.call-start
  73.0 0.5 all-gather.3.cloned.1.call-update
  73.5 0.7 broadcast_compare_fusion
  74.2 0.1 convert_reduce_fusion
  74.3 0.2 fusion.34
  74.6 14.3 %reduce-scatter.2.cloned.1.call-done = bf16[32,4608]{1,0:T(8,128)(2,1)} async-done(((bf16[64,4608]{1,0:T(8,128)(2,1)}), bf16[32,4608]{1,0:T(8,128)(2,1)}) %reduce-scatter.2.cloned.1.call-update) | async-done | bytes 294928 | tf_op jit(solution)/shard_map/reduce_scatter | solution.py:104
  88.9 1.1 reshape.203
  90.0 0.2 multiply_reduce_fusion
  90.3 40.3 %all-gather.5.cloned.1.call-done = bf16[1152,1152]{1,0:T(8,128)(2,1)} async-done(((bf16[288,1152]{1,0:T(8,128)(2,1)}), bf16[1152,1152]{1,0:T(8,128)(2,1)}) %all-gather.5.cloned.1.call-update) | async-done | bytes 2654224 | tf_op jit(solution)/shard_map/all_gather | solution.py:64
  130.6 2.7 fusion.3
  133.3 0.9 copy.42
  134.2 3.5 %all-to-all-start.2 = ((bf16[1,16,72,128]{3,2,0,1:T(8,128)(2,1)}), bf16[1,16,72,128]{3,2,0,1:T(8,128)(2,1)S(1)}, u32[]{:S(2)}, u32[]{:S(2)}) async-start(bf16[1,16,72,128]{3,2,0,1:T(8,128)(2,1)} %bitcast.12), calls=%async_computation.3 | async-start | bytes 589824 | tf_op jit(solution)/shard_map/all_to_all | solution.py:121
  137.7 135.5 %all-gather.3.cloned.1.call-done = bf16[1152,3456]{1,0:T(8,128)(2,1)} async-done(((bf16[288,3456]{1,0:T(8,128)(2,1)}), bf16[1152,3456]{1,0:T(8,128)(2,1)}) %all-gather.3.cloned.1.call-update) | async-done | bytes 7962640 | tf_op jit(solution)/shard_map/all_gather | solution.py:63
  273.2 4.7 %fusion.1 = bf16[3456,128]{0,1:T(8,128)(2,1)S(1)} fusion(bf16[1152,3456]{1,0:T(8,128)(2,1)} %all-gather.3.cloned.1.call-done, bf16[128,1152]{1,0:T(8,128)(2,1)S(1)} %copy-done.3, f32[1152]{0:T(1024)S(1)} %copy-done.8, f32[1152]{0:T(1024)S(1)} %copy-done.6, f32[128]{0:T(128)S(1)} %add_rsqrt_fusion, f32[128]{0:T(128)S(1)} %broadcast_multiply_fusion.2), kind=kOutput, calls=%fused_computation.4 | convolution fusion | flops 1020542976 | bytes 9152512 | tf_op jit(solution)/shard_map/dot_general | solution.py:68
  278.0 1.0 copy.39
  279.0 1.1 copy.40
  280.1 3.7 %all-to-all-start.1 = ((bf16[3,16,72,128]{3,2,0,1:T(8,128)(2,1)}), bf16[3,16,72,128]{3,2,0,1:T(8,128)(2,1)S(1)}, u32[]{:S(2)}, u32[]{:S(2)}) async-start(bf16[3,16,72,128]{3,2,0,1:T(8,128)(2,1)} %copy.40), calls=%async_computation.2 | async-start | bytes 1769472 | tf_op jit(solution)/shard_map/all_to_all | solution.py:120
  283.8 0.1 fusion.53
  283.9 0.1 and_and_fusion
  284.0 0.3 copy.55
  284.4 0.2 reshape.200
  284.6 11.3 %all-to-all-done.1 = bf16[3,16,72,128]{3,2,0,1:T(8,128)(2,1)S(1)} async-done(((bf16[3,16,72,128]{3,2,0,1:T(8,128)(2,1)}), bf16[3,16,72,128]{3,2,0,1:T(8,128)(2,1)S(1)}, u32[]{:S(2)}, u32[]{:S(2)}) %all-to-all-start.1) | async-done | bytes 884768 | tf_op jit(solution)/shard_map/all_to_all | solution.py:120
  295.9 0.9 copy.54
  296.8 0.6 fusion.62
  297.4 0.2 reshape.199
  297.6 0.2 squeeze.21
  297.8 0.0 copy-start.4
  297.8 0.2 squeeze.24
  298.0 0.7 fusion.63
  298.8 0.2 divide_convert_fusion
  299.0 0.4 fusion.14
  299.4 1.9 fusion.64
  301.3 3.0 fusion.12
  304.3 3.1 fusion.13
  307.4 0.1 pad_maximum_fusion
  307.5 0.2 slice_bitcast_fusion.1
  307.7 0.1 pad_maximum_fusion.1
  307.8 13.9 %all_to_all.40 = bf16[2,3,8,72,128]{4,3,2,1,0:T(8,128)(2,1)S(1)} all-to-all(bf16[2,3,8,72,128]{4,3,2,1,0:T(8,128)(2,1)S(1)} %pad_maximum_fusion.1), channel_id=1, replica_groups=mesh['section'=4,'vit'=2,'dp'=4] {'vit'}, dimensions={0} | all-to-all | bytes 1769472 | tf_op jit(solution)/shard_map/all_to_all | solution.py:194
  321.6 0.1 copy.48
  321.7 0.0 copy-start.1
  321.7 6.0 %fusion.61 = (f32[128]{0:T(128)S(1)}, f32[128]{0:T(128)S(1)}, f32[128,1152]{1,0:T(8,128)S(1)}) fusion(f32[128]{0:T(128)S(1)} %add_rsqrt_fusion, f32[128]{0:T(128)S(1)} %broadcast_multiply_fusion.2, bf16[128,1152]{1,0:T(8,128)(2,1)S(1)} %copy-done.3, f32[1152]{0:T(1024)S(1)} %copy-done.6, bf16[3456,128]{1,0:T(8,128)(2,1)S(1)} %bitcast.64, ...), kind=kOutput, calls=%fused_computation.106 | convolution fusion | flops 1020247808 | bytes 9738752 | tf_op jit(solution)/shard_map/dot_general | solution.py:200
  327.7 1.1 fusion.33
  (35 shorter events, 0.1 us)
Async XLA Ops:
  7.4 7.5 %copy-start = (s32[4,2]{0,1:T(2,128)S(1)}, s32[4,2]{0,1:T(2,128)}, u32[]{:S(2)}) copy-start(s32[4,2]{0,1:T(2,128)} %param.17) | copy-start | bytes 100
  7.4 8.5 %copy-start.2 = (bf16[128,1152]{1,0:T(8,128)(2,1)S(1)}, bf16[128,1152]{1,0:T(8,128)(2,1)}, u32[]{:S(2)}) copy-start(bf16[128,1152]{1,0:T(8,128)(2,1)} %param.20) | copy-start | bytes 884740
  7.4 8.8 %copy-start.10 = (s32[2,128]{1,0:T(2,128)S(1)}, s32[2,128]{1,0:T(2,128)}, u32[]{:S(2)}) copy-start(s32[2,128]{1,0:T(2,128)} %param.16) | copy-start | bytes 3076
  7.4 8.9 %copy-start.9 = (f32[1152]{0:T(1024)S(1)}, f32[1152]{0:T(1024)}, u32[]{:S(2)}) copy-start(f32[1152]{0:T(1024)} %param.26) | copy-start | bytes 13828
  7.4 8.9 %copy-start.5 = (f32[1152]{0:T(1024)S(1)}, f32[1152]{0:T(1024)}, u32[]{:S(2)}) copy-start(f32[1152]{0:T(1024)} %param.25) | copy-start | bytes 13828
  7.4 26.8 %copy-start.11 = (s32[4]{0:T(128)S(1)}, s32[4]{0:T(128)}, u32[]{:S(2)}) copy-start(s32[4]{0:T(128)} %param.18) | copy-start | bytes 52
  7.4 26.8 %copy-start.7 = (f32[2304]{0:T(1024)S(1)}, f32[2304]{0:T(1024)}, u32[]{:S(2)}) copy-start(f32[2304]{0:T(1024)} %param.28) | copy-start | bytes 27652
  7.4 35.8 %all-to-all-start = ((bf16[8,16,4096]{2,1,0:T(8,128)(2,1)}), bf16[8,16,4096]{2,1,0:T(8,128)(2,1)S(1)}, u32[]{:S(2)}, u32[]{:S(2)}) async-start(bf16[8,16,4096]{2,1,0:T(8,128)(2,1)} %bitcast.71), calls=%async_computation | async-start | bytes 2097152 | tf_op jit(solution)/shard_map/all_to_all | solution.py:81
  14.8 74.0 %reduce-scatter.2.cloned.1.call-start = ((), (), s32[]{:S(2)}) async-start(), calls=%async_computation.5 | async-start | bytes 884736 | tf_op jit(solution)/shard_map/reduce_scatter | solution.py:104
  72.3 1.9 copy-start.3
  72.4 58.2 %all-gather.5.cloned.1.call-start = ((), (), s32[]{:S(2)}) async-start(), calls=%async_computation.7 | async-start | bytes 3317760 | tf_op jit(solution)/shard_map/all_gather | solution.py:64
  72.9 200.3 %all-gather.3.cloned.1.call-start = ((), (), s32[]{:S(2)}) async-start(), calls=%async_computation.6 | async-start | bytes 9953280 | tf_op jit(solution)/shard_map/all_gather | solution.py:63
  130.6 142.6 %copy-start.6 = (f32[1152]{0:T(1024)S(1)}, f32[1152]{0:T(1024)}, u32[]{:S(2)}) copy-start(f32[1152]{0:T(1024)} %param.21) | copy-start | bytes 13828
  130.6 142.6 %copy-start.8 = (f32[1152]{0:T(1024)S(1)}, f32[1152]{0:T(1024)}, u32[]{:S(2)}) copy-start(f32[1152]{0:T(1024)} %param.22) | copy-start | bytes 13828
  134.2 145.8 %all-to-all-start.2 = ((bf16[1,16,72,128]{3,2,0,1:T(8,128)(2,1)}), bf16[1,16,72,128]{3,2,0,1:T(8,128)(2,1)S(1)}, u32[]{:S(2)}, u32[]{:S(2)}) async-start(bf16[1,16,72,128]{3,2,0,1:T(8,128)(2,1)} %bitcast.12), calls=%async_computation.3 | async-start | bytes 589824 | tf_op jit(solution)/shard_map/all_to_all | solution.py:121
  280.1 15.8 %all-to-all-start.1 = ((bf16[3,16,72,128]{3,2,0,1:T(8,128)(2,1)}), bf16[3,16,72,128]{3,2,0,1:T(8,128)(2,1)S(1)}, u32[]{:S(2)}, u32[]{:S(2)}) async-start(bf16[3,16,72,128]{3,2,0,1:T(8,128)(2,1)} %copy.40), calls=%async_computation.2 | async-start | bytes 1769472 | tf_op jit(solution)/shard_map/all_to_all | solution.py:120
  297.8 0.9 copy-start.4
  321.7 7.2 %copy-start.1 = (s32[4,2]{0,1:T(2,128)S(1)}, s32[4,2]{0,1:T(2,128)}, u32[]{:S(2)}) copy-start(s32[4,2]{0,1:T(2,128)} %param.17) | copy-start | bytes 100
Sparse Core Ops, SparseCore 0:
  72.5 16.3 reduce-scatter.1
Sparse Core Ops, SparseCore 1:
  74.4 56.1 all-gather.4
  132.1 141.1 all-gather.2
